TPU v7x, 512 devices: a whole 4x8x8 slice. The times are simulated.
512 devices in a mesh: dp: 16 (over z_lo, y), mp: 8 (over z_hi, core), section: 4 (over x).
Axes of the slice: x: 4, y: 8, z: 8 (z_hi: 4, z_lo: 2; z = z_hi * 2 + z_lo), core: 2. Of those that a mesh axis runs over, the one named last changes fastest.
Arguments:
- states: bfloat16 [16384, 8192], P(('dp', 'section'), 'mp'), may hold values from -6 to 6
- direction: bfloat16 [16384, 1024], P(('dp', 'section'), 'mp'), may hold values from -0.09375 to 0.09375
- old_logp: bfloat16 [16384], P(('dp', 'section')), may hold values from -4 to -0.049804688
- lengths: int32 [128], P(('dp', 'section')), may hold values from 1 to 128, as said below
- group_ids: int32 [128], P(('dp', 'section')), may hold values from 0 to 15, as said below
- routes: int32 [16384, 1], P(('dp', 'section')), may hold values from 0 to 15; in each aligned block of 256 rows (0 to 255, 256 to 511, ...) at most 20 rows name the same one
- reward_head: bfloat16 [8192], P('mp'), may hold values from -0.0625 to 0.0625
- policy_k: bfloat16 [8192, 1024], P(('dp', 'section'), 'mp'), may hold values from -0.0625 to 0.0625
- reference_k: bfloat16 [8192, 1024], P(('dp', 'section'), 'mp'), may hold values from -0.0625 to 0.0625
Outputs:
- grad_k: float32 [8192, 1024], P(('dp', 'section'), 'mp')
- packed_logp: float32 [16, 4, 320], P('dp', 'section')
Inputs may be any that keep to these rules, and one draw needn't show every extreme that they name: `lengths`: some response has all 128 tokens valid. `group_ids`: each prompt id is held by exactly 8 responses. `routes`: among the rows of one rollout device at most 20 name the same learner shard, a bound that some block reaches of them.
All inputs are finite; a program needn't handle non-finite values.
Results may differ from a plain program's by a relative error of at most 0.004.
Values may be sent and summed in bfloat16 or wider, within the bound.
No kernel may reach another device: no remote copies, remote signals or barrier semaphores. Data moves between devices by JAX's collectives and lax.ppermute only.
A program may use at most 64 MiB of HBM per device.

v0:
```python
import jax
import jax.numpy as jnp
from jax import lax
from jax.sharding import PartitionSpec as P

GROUP = 8
kl_weight = 0.4
var_offset = 0.25


def row_slots(routes, shards, capacity):
    target = routes[:, 0]
    choose = (target[:, None] == jnp.arange(shards, dtype=jnp.int32)[None, :]).astype(jnp.int32)
    ranked = jnp.cumsum(choose, axis=0) - 1
    within = jnp.sum(ranked * choose, axis=1)
    places = target * capacity + within
    row_count = routes.shape[0]
    source = jnp.full((shards * capacity,), row_count, jnp.int32)
    return source.at[places].set(jnp.arange(row_count, dtype=jnp.int32))


def pick_rows(values, source):
    return jnp.take(values, source, axis=0, mode="fill", fill_value=0)


def advantages(scores, lengths, group_ids):
    seq_count = lengths.shape[0]
    seq_len = scores.shape[0] // seq_count
    groups = seq_count * lax.axis_size("dp") * lax.axis_size("section") // GROUP
    valid = (jnp.arange(seq_len, dtype=jnp.int32)[None, :] < lengths[:, None]).astype(jnp.float32)
    reward = jnp.sum(scores.reshape(seq_count, seq_len) * valid, axis=1) / jnp.sqrt(
        lengths.astype(jnp.float32)
    )
    member = (group_ids[:, None] == jnp.arange(groups, dtype=jnp.int32)[None, :]).astype(
        jnp.float32
    )
    totals, squares = lax.psum(
        (
            jnp.sum(member * reward[:, None], axis=0),
            jnp.sum(member * (reward * reward)[:, None], axis=0),
        ),
        ("dp", "section"),
    )
    center = totals / GROUP
    spread = squares / GROUP - center * center
    own_center = jnp.sum(member * center[None, :], axis=1)
    own_spread = jnp.sum(member * spread[None, :], axis=1)
    advantage = ((reward - own_center) / jnp.sqrt(own_spread + var_offset)).astype(jnp.bfloat16)
    return (jnp.repeat(advantage, seq_len), valid.reshape(-1))


def project(whole, policy_k, reference_k):
    return (
        jnp.dot(
            whole,
            lax.all_gather(policy_k, ("dp", "section"), axis=0, tiled=True),
            preferred_element_type=jnp.float32,
        ),
        jnp.dot(
            whole,
            lax.all_gather(reference_k, ("dp", "section"), axis=0, tiled=True),
            preferred_element_type=jnp.float32,
        ),
    )


def token_coef(dir_rows, old_rows, adv_rows, valid_rows, term_policy, term_reference):
    logp = old_rows.astype(jnp.float32) + term_policy
    coef = valid_rows * (
        -adv_rows * jnp.exp(term_policy) + kl_weight * (1.0 - jnp.exp(term_reference - term_policy))
    )
    change = (coef[:, None] * dir_rows.astype(jnp.float32)).astype(jnp.bfloat16)
    return (logp, change)


def weight_grads(whole, change):
    return lax.psum_scatter(
        lax.dot_general(
            whole, change, (((0,), (0,)), ((), ())), preferred_element_type=jnp.float32
        ),
        ("dp", "section"),
        scatter_dimension=0,
        tiled=True,
    )


def body(
    states, direction, old_logp, lengths, group_ids, routes, reward_head, policy_k, reference_k
):
    row_count = states.shape[0]
    score_part = jnp.dot(states, reward_head, preferred_element_type=jnp.float32)
    shards = lax.axis_size("dp")
    capacity = max(2, 5 * row_count // (4 * shards))
    source = row_slots(routes, shards, capacity)
    scores = lax.psum(score_part, "mp")
    adv_rows, valid_rows = advantages(scores, lengths, group_ids)
    extras = jnp.stack([old_logp, adv_rows, valid_rows.astype(jnp.bfloat16)], axis=1)
    send_states = pick_rows(states, source).reshape(shards, capacity, states.shape[1])
    send_dir = pick_rows(direction, source).reshape(shards, capacity, direction.shape[1])
    send_extras = pick_rows(extras, source).reshape(shards, capacity, 3)
    got_states, got_dir, got_extras = (
        lax.all_to_all(send_states, "dp", split_axis=0, concat_axis=0, tiled=True),
        lax.all_to_all(send_dir, "dp", split_axis=0, concat_axis=0, tiled=True),
        lax.all_to_all(send_extras, "dp", split_axis=0, concat_axis=0, tiled=True),
    )
    slot_count = shards * capacity
    learn_states = got_states.reshape(slot_count, states.shape[1])
    learn_dir = got_dir.reshape(slot_count, direction.shape[1])
    learn_extras = got_extras.reshape(slot_count, 3)
    whole = lax.all_gather(learn_states, "mp", axis=1, tiled=True)
    key_policy, key_reference = project(whole, policy_k, reference_k)
    dir_wide = learn_dir.astype(jnp.float32)
    term_policy, term_reference = lax.psum(
        (jnp.sum(dir_wide * key_policy, axis=1), jnp.sum(dir_wide * key_reference, axis=1)), "mp"
    )
    logp, change = token_coef(
        learn_dir,
        learn_extras[:, 0],
        learn_extras[:, 1].astype(jnp.float32),
        learn_extras[:, 2].astype(jnp.float32),
        term_policy,
        term_reference,
    )
    grad_k = weight_grads(whole, change)
    packed_logp = logp.reshape(1, 1, slot_count)
    return (grad_k, packed_logp)


def solution(mesh):
    return jax.shard_map(
        body,
        mesh=mesh,
        in_specs=(
            P(("dp", "section"), "mp"),
            P(("dp", "section"), "mp"),
            P(("dp", "section")),
            P(("dp", "section")),
            P(("dp", "section")),
            P(("dp", "section"), None),
            P("mp"),
            P(("dp", "section"), "mp"),
            P(("dp", "section"), "mp"),
        ),
        out_specs=(P(("dp", "section"), "mp"), P("dp", "section", None)),
        check_vma=False,
    )
```

profile of v0, /device:TPU:64, one launch (start us, length us, event | category | flops | bytes accessed | tf_op | source)
XLA Modules:
  0.0 1203.8 jit_solution(4523003245266882236)
XLA Ops:
  7.2 0.0 copy-start
  7.2 0.0 all-gather.6.cloned.1.call-start
  7.2 0.7 all-gather.6.cloned.1.call-update
  7.9 0.0 all-gather.4.cloned.1.call-start
  8.0 0.7 fusion.6
  8.6 0.6 reduce-window.6
  9.2 0.2 slice_reduce_fusion
  9.4 0.8 fusion.5
  10.2 0.7 compare_select_fusion
  10.9 1.4 scatter_custom_fusion
  12.3 0.0 copy-done
  12.3 0.0 copy-start.1
  12.4 2.1 gather_fusion
  14.5 0.0 copy-start.2
  14.5 0.0 copy-start.5
  14.5 0.0 copy-start.4
  14.5 0.1 gather.19
  14.6 0.1 broadcast_in_dim.52
  14.7 0.1 broadcast_select_fusion
  14.9 29.1 %all_to_all.15 = bf16[16,20,1024]{2,1,0:T(8,128)(2,1)S(1)} all-to-all(bf16[16,20,1024]{2,1,0:T(8,128)(2,1)S(1)} %broadcast_select_fusion), channel_id=1, replica_groups=mesh['dp'=16,'mp'=8,'section'=4] {'dp'}, dimensions={0} | all-to-all | bytes 1310720 | tf_op jit(solution)/shard_map/all_to_all | solution.py:102
  44.0 1.0 reshape.105
  45.0 0.0 all-gather.4.cloned.1.call-update
  45.0 0.0 all-gather.8.cloned.1.call-start
  45.0 0.7 all-gather.8.cloned.1.call-update
  45.7 0.0 copy-done.1
  45.7 1.4 gather_fusion.2
  47.2 0.8 broadcast_select_fusion.1
  47.9 6.3 all-to-all-start.2
  54.3 0.0 reduce-scatter.2.cloned.1.call-start
  54.3 0.0 copy-done.2
  54.3 0.0 copy-done.5
  54.4 0.2 fusion.16
  54.6 0.0 copy-done.4
  54.6 0.1 fusion.13
  54.7 7.0 all-to-all-done.2
  61.7 253.6 %all-gather.6.cloned.1.call-done = bf16[8192,128]{1,0:T(8,128)(2,1)} async-done(((bf16[128,128]{1,0:T(8,128)(2,1)}), bf16[8192,128]{1,0:T(8,128)(2,1)}) %all-gather.6.cloned.1.call-update) | async-done | bytes 2097168 | tf_op jit(solution)/shard_map/all_gather | solution.py:56
  315.3 65.4 %all-gather.4.cloned.1.call-done = bf16[320,8192]{1,0:T(8,128)(2,1)} async-done(((bf16[320,1024]{1,0:T(8,128)(2,1)}), bf16[320,8192]{1,0:T(8,128)(2,1)}) %all-gather.4.cloned.1.call-update) | async-done | bytes 5242896 | tf_op jit(solution)/shard_map/all_gather | solution.py:110
  380.7 4.8 fusion
  385.5 0.0 copy-start.3
  385.5 297.1 %all-gather.8.cloned.1.call-done = bf16[8192,128]{1,0:T(8,128)(2,1)} async-done(((bf16[128,128]{1,0:T(8,128)(2,1)}), bf16[8192,128]{1,0:T(8,128)(2,1)}) %all-gather.8.cloned.1.call-update) | async-done | bytes 2097168 | tf_op jit(solution)/shard_map/all_gather | solution.py:61
  682.6 4.8 fusion.1
  687.4 14.7 %all-reduce.1 = (f32[2,128]{1,0:T(2,128)S(1)}, f32[320]{0:T(512)S(1)}, f32[320]{0:T(512)S(1)}) all-reduce(f32[2,128]{1,0:T(2,128)S(1)} %bitcast.47, f32[320]{0:T(512)S(1)} %fusion.1, f32[320]{0:T(512)S(1)} %fusion), channel_id=1, replica_groups=mesh['dp'=16,'mp'=8,'section'=4] {'mp'}, use_global_device_ids=true, to_apply=%region_4.5 | all-reduce | flops 896 | bytes 7168 | tf_op jit(solution)/shard_map/psum | solution.py:95
  702.1 0.2 select_reduce_fusion.4
  702.3 0.0 copy-done.3
  702.3 0.1 select_reduce_fusion.3
  702.4 157.2 %all-reduce = (f32[16]{0:T(128)S(1)}, f32[16]{0:T(128)S(1)}) all-reduce(f32[16]{0:T(128)S(1)} %get-tuple-element.7, f32[16]{0:T(128)S(1)} %get-tuple-element.8), channel_id=1, replica_groups=mesh['dp'=16,'mp'=8,'section'=4] {'dp','section'}, use_global_device_ids=true, to_apply=%region_7.8 | all-reduce | flops 32 | bytes 256 | tf_op jit(solution)/shard_map/psum | solution.py:37
  859.6 0.2 select_reduce_fusion.2
  859.8 0.1 broadcast_bitcast_fusion
  859.9 0.1 copy.22
  860.1 1.4 gather_fusion.1
  861.5 0.1 copy.23
  861.6 0.1 gather.21
  861.7 10.8 all_to_all.16
  872.5 0.1 reshape.107
  872.7 6.5 fusion.2
  879.1 0.0 reduce-scatter.2.cloned.1.call-update
  879.1 0.6 reshape.108
  879.7 317.5 %reduce-scatter.2.cloned.1.call-done = f32[128,128]{1,0:T(8,128)} async-done(((f32[8192,128]{1,0:T(8,128)}), f32[128,128]{1,0:T(8,128)}) %reduce-scatter.2.cloned.1.call-update) | async-done | bytes 65552 | tf_op jit(solution)/shard_map/reduce_scatter | solution.py:77
  (20 shorter events, 0.2 us)
Async XLA Ops:
  7.2 5.2 copy-start
  7.2 308.1 %all-gather.6.cloned.1.call-start = ((), (), s32[]{:S(2)}) async-start(), calls=%async_computation.5 | async-start | bytes 2129920 | tf_op jit(solution)/shard_map/all_gather | solution.py:56
  7.9 372.8 %all-gather.4.cloned.1.call-start = ((), (), s32[]{:S(2)}) async-start(), calls=%async_computation.4 | async-start | bytes 5898240 | tf_op jit(solution)/shard_map/all_gather | solution.py:110
  12.3 33.4 %copy-start.1 = (bf16[256,128]{1,0:T(8,128)(2,1)S(1)}, bf16[256,128]{1,0:T(8,128)(2,1)}, u32[]{:S(2)}) copy-start(bf16[256,128]{1,0:T(8,128)(2,1)} %param.10) | copy-start | bytes 196612
  14.5 39.9 %copy-start.2 = (bf16[1024]{0:T(1024)(128)(2,1)S(1)}, bf16[1024]{0:T(1024)(128)(2,1)}, u32[]{:S(2)}) copy-start(bf16[1024]{0:T(1024)(128)(2,1)} %param.15) | copy-start | bytes 6148
  14.5 39.9 %copy-start.5 = (bf16[256]{0:T(256)(128)(2,1)S(1)}, bf16[256]{0:T(256)(128)(2,1)}, u32[]{:S(2)}) copy-start(bf16[256]{0:T(256)(128)(2,1)} %param.11) | copy-start | bytes 1540
  14.5 40.1 %copy-start.4 = (s32[2]{0:T(128)S(1)}, s32[2]{0:T(128)}, u32[]{:S(2)}) copy-start(s32[2]{0:T(128)} %param.12) | copy-start | bytes 28
  45.0 637.6 %all-gather.8.cloned.1.call-start = ((), (), s32[]{:S(2)}) async-start(), calls=%async_computation.6 | async-start | bytes 2129920 | tf_op jit(solution)/shard_map/all_gather | solution.py:61
  47.9 13.8 %all-to-all-start.2 = ((bf16[16,20,128]{2,1,0:T(8,128)(2,1)}), bf16[16,20,128]{2,1,0:T(8,128)(2,1)S(1)}, u32[]{:S(2)}, u32[]{:S(2)}) async-start(bf16[16,20,128]{2,1,0:T(8,128)(2,1)} %broadcast_select_fusion.1), calls=%async_computation.2 | async-start | bytes 196608 | tf_op jit(solution)/shard_map/all_to_all | solution.py:103
  54.3 1143.0 %reduce-scatter.2.cloned.1.call-start = ((), (), s32[]{:S(2)}) async-start(), calls=%async_computation.7 | async-start | bytes 4259840 | tf_op jit(solution)/shard_map/reduce_scatter | solution.py:77
  385.5 316.8 %copy-start.3 = (s32[2]{0:T(128)S(1)}, s32[2]{0:T(128)}, u32[]{:S(2)}) copy-start(s32[2]{0:T(128)} %param.13) | copy-start | bytes 28
Sparse Core Ops, SparseCore 0:
  10.1 305.1 all-gather.5
  317.4 63.2 all-gather.3
  382.8 299.7 all-gather.7
  879.3 317.9 reduce-scatter.1
where the time goes:
time: 1200 us
  waiting for transfers between devices  942 us (78%)
  blocking collectives  212 us (18%)
  matrix products  16.2 us (1%)
  between operations  14 us (1%)
    reduce_scatter x1, waiting for transfers between devices, weight_grads(): lax.psum_scatter(lax.dot_general(whole, change, (((0,), (0,)), ((), ())),...  318 us
    all_gather x1, waiting for transfers between devices, project(): lax.all_gather(reference_k, ('dp', 'section'), axis=0, tiled=True)  297 us
    all_gather x1, waiting for transfers between devices, project(): lax.all_gather(policy_k, ('dp', 'section'), axis=0, tiled=True)  254 us
    psum x1, blocking collectives, advantages(): lax.psum((jnp.sum(member * reward[:, None], axis=0), jnp.sum(member * (re...  157 us
    all_gather x1, waiting for transfers between devices, body(): whole = lax.all_gather(learn_states, 'mp', axis=1, tiled=True)  65.4 us
    all_to_all x1, blocking collectives, body(): lax.all_to_all(send_states, 'dp', split_axis=0, concat_axis=0, tiled=True)  29.1 us
  transfers between devices with their start and end apart: 5, of which 5 were waited for; matrix products, arithmetic and copies ran while one was open for 1% of the time, Pallas kernels for 0%

commit v1 on v0

--- a/solution.py
+++ b/solution.py
@@ -35,11 +35,14 @@
         jnp.float32
     )
     totals, squares = lax.psum(
-        (
-            jnp.sum(member * reward[:, None], axis=0),
-            jnp.sum(member * (reward * reward)[:, None], axis=0),
+        lax.psum(
+            (
+                jnp.sum(member * reward[:, None], axis=0),
+                jnp.sum(member * (reward * reward)[:, None], axis=0),
+            ),
+            "section",
         ),
-        ("dp", "section"),
+        "dp",
     )
     center = totals / GROUP
     spread = squares / GROUP - center * center

time: 1200 us -> 1090 us (0.908)
  the two profiles are of different devices: /device:TPU:64 before, /device:TPU:128 now
where the time goes in v1:
time: 1090 us
  waiting for transfers between devices  944 us (87%)
  blocking collectives  97.5 us (9%)
  matrix products  16.2 us (1%)
  between operations  14 us (1%)
    reduce_scatter x1, waiting for transfers between devices, weight_grads(): lax.psum_scatter(lax.dot_general(whole, change, (((0,), (0,)), ((), ())),...  320 us
    all_gather x1, waiting for transfers between devices, project(): lax.all_gather(reference_k, ('dp', 'section'), axis=0, tiled=True)  298 us
    all_gather x1, waiting for transfers between devices, project(): lax.all_gather(policy_k, ('dp', 'section'), axis=0, tiled=True)  253 us
    all_gather x1, waiting for transfers between devices, body(): whole = lax.all_gather(learn_states, 'mp', axis=1, tiled=True)  64.4 us
    psum x1, blocking collectives, advantages(): lax.psum(lax.psum((jnp.sum(member * reward[:, None], axis=0), jnp.sum(mem...  35.4 us
    all_to_all x1, blocking collectives, body(): lax.all_to_all(send_states, 'dp', split_axis=0, concat_axis=0, tiled=True)  30.2 us
  transfers between devices with their start and end apart: 5, of which 5 were waited for; matrix products, arithmetic and copies ran while one was open for 1% of the time, Pallas kernels for 0%

profile of v1, /device:TPU:128, one launch (start us, length us, event | category | flops | bytes accessed | tf_op | source)
XLA Modules:
  0.0 1091.3 jit_solution(8042205743395202685)
XLA Ops:
  7.2 0.0 copy-start
  7.2 0.0 all-gather.6.cloned.1.call-start
  7.2 0.7 all-gather.6.cloned.1.call-update
  7.9 0.0 all-gather.4.cloned.1.call-start
  8.0 0.7 fusion.6
  8.6 0.6 reduce-window.6
  9.2 0.2 slice_reduce_fusion
  9.4 0.8 fusion.5
  10.2 0.7 compare_select_fusion
  10.9 1.4 scatter_custom_fusion
  12.3 0.0 copy-done
  12.3 0.0 copy-start.1
  12.4 2.1 gather_fusion
  14.5 0.0 copy-start.2
  14.5 0.0 copy-start.5
  14.5 0.0 copy-start.4
  14.5 0.1 gather.19
  14.6 0.1 broadcast_in_dim.52
  14.7 0.1 broadcast_select_fusion
  14.9 30.2 %all_to_all.15 = bf16[16,20,1024]{2,1,0:T(8,128)(2,1)S(1)} all-to-all(bf16[16,20,1024]{2,1,0:T(8,128)(2,1)S(1)} %broadcast_select_fusion), channel_id=1, replica_groups=mesh['dp'=16,'mp'=8,'section'=4] {'dp'}, dimensions={0} | all-to-all | bytes 1310720 | tf_op jit(solution)/shard_map/all_to_all | solution.py:105
  45.1 1.0 reshape.105
  46.0 0.0 all-gather.4.cloned.1.call-update
  46.1 0.0 all-gather.8.cloned.1.call-start
  46.1 0.7 all-gather.8.cloned.1.call-update
  46.8 0.0 copy-done.1
  46.8 1.4 gather_fusion.2
  48.3 0.8 broadcast_select_fusion.1
  49.0 5.9 all-to-all-start.2
  54.9 0.0 reduce-scatter.2.cloned.1.call-start
  55.0 0.0 copy-done.2
  55.0 0.0 copy-done.5
  55.0 0.2 fusion.16
  55.2 0.0 copy-done.4
  55.2 0.1 fusion.13
  55.3 8.2 all-to-all-done.2
  63.5 252.7 %all-gather.6.cloned.1.call-done = bf16[8192,128]{1,0:T(8,128)(2,1)} async-done(((bf16[128,128]{1,0:T(8,128)(2,1)}), bf16[8192,128]{1,0:T(8,128)(2,1)}) %all-gather.6.cloned.1.call-update) | async-done | bytes 2097168 | tf_op jit(solution)/shard_map/all_gather | solution.py:59
  316.1 64.4 %all-gather.4.cloned.1.call-done = bf16[320,8192]{1,0:T(8,128)(2,1)} async-done(((bf16[320,1024]{1,0:T(8,128)(2,1)}), bf16[320,8192]{1,0:T(8,128)(2,1)}) %all-gather.4.cloned.1.call-update) | async-done | bytes 5242896 | tf_op jit(solution)/shard_map/all_gather | solution.py:113
  380.6 4.8 fusion
  385.4 0.0 copy-start.3
  385.4 297.6 %all-gather.8.cloned.1.call-done = bf16[8192,128]{1,0:T(8,128)(2,1)} async-done(((bf16[128,128]{1,0:T(8,128)(2,1)}), bf16[8192,128]{1,0:T(8,128)(2,1)}) %all-gather.8.cloned.1.call-update) | async-done | bytes 2097168 | tf_op jit(solution)/shard_map/all_gather | solution.py:64
  683.0 4.8 fusion.1
  687.8 12.6 %all-reduce.1 = (f32[2,128]{1,0:T(2,128)S(1)}, f32[320]{0:T(512)S(1)}, f32[320]{0:T(512)S(1)}) all-reduce(f32[2,128]{1,0:T(2,128)S(1)} %bitcast.47, f32[320]{0:T(512)S(1)} %fusion.1, f32[320]{0:T(512)S(1)} %fusion), channel_id=1, replica_groups=mesh['dp'=16,'mp'=8,'section'=4] {'mp'}, use_global_device_ids=true, to_apply=%region_4.5 | all-reduce | flops 896 | bytes 7168 | tf_op jit(solution)/shard_map/psum | solution.py:98
  700.4 0.2 select_reduce_fusion.4
  700.6 0.0 copy-done.3
  700.6 0.1 select_reduce_fusion.3
  700.7 8.3 all-reduce.2
  709.0 35.4 %all-reduce = (f32[16]{0:T(128)S(1)}, f32[16]{0:T(128)S(1)}) all-reduce(f32[16]{0:T(128)S(1)} %get-tuple-element.14, f32[16]{0:T(128)S(1)} %get-tuple-element.15), channel_id=1, replica_groups=mesh['dp'=16,'mp'=8,'section'=4] {'dp'}, use_global_device_ids=true, to_apply=%region_8.9 | all-reduce | flops 32 | bytes 256 | tf_op jit(solution)/shard_map/psum | solution.py:37
  744.3 0.2 select_reduce_fusion.2
  744.5 0.1 broadcast_bitcast_fusion
  744.6 0.1 copy.22
  744.8 1.4 gather_fusion.1
  746.2 0.1 copy.23
  746.3 0.1 gather.21
  746.4 11.0 %all_to_all.16 = bf16[16,20,3]{1,2,0:T(4,128)(2,1)S(1)} all-to-all(bf16[16,20,3]{1,2,0:T(4,128)(2,1)S(1)} %copy.24), channel_id=1, replica_groups=mesh['dp'=16,'mp'=8,'section'=4] {'dp'}, dimensions={0} | all-to-all | bytes 3840 | tf_op jit(solution)/shard_map/all_to_all | solution.py:107
  757.5 0.1 reshape.107
  757.6 6.5 fusion.2
  764.1 0.0 reduce-scatter.2.cloned.1.call-update
  764.1 0.6 reshape.108
  764.7 320.1 %reduce-scatter.2.cloned.1.call-done = f32[128,128]{1,0:T(8,128)} async-done(((f32[8192,128]{1,0:T(8,128)}), f32[128,128]{1,0:T(8,128)}) %reduce-scatter.2.cloned.1.call-update) | async-done | bytes 65552 | tf_op jit(solution)/shard_map/reduce_scatter | solution.py:80
  (20 shorter events, 0.2 us)
Async XLA Ops:
  7.2 5.2 copy-start
  7.2 309.0 %all-gather.6.cloned.1.call-start = ((), (), s32[]{:S(2)}) async-start(), calls=%async_computation.5 | async-start | bytes 2129920 | tf_op jit(solution)/shard_map/all_gather | solution.py:59
  7.9 372.7 %all-gather.4.cloned.1.call-start = ((), (), s32[]{:S(2)}) async-start(), calls=%async_computation.4 | async-start | bytes 5898240 | tf_op jit(solution)/shard_map/all_gather | solution.py:113
  12.3 34.5 %copy-start.1 = (bf16[256,128]{1,0:T(8,128)(2,1)S(1)}, bf16[256,128]{1,0:T(8,128)(2,1)}, u32[]{:S(2)}) copy-start(bf16[256,128]{1,0:T(8,128)(2,1)} %param.10) | copy-start | bytes 196612
  14.5 40.5 %copy-start.2 = (bf16[1024]{0:T(1024)(128)(2,1)S(1)}, bf16[1024]{0:T(1024)(128)(2,1)}, u32[]{:S(2)}) copy-start(bf16[1024]{0:T(1024)(128)(2,1)} %param.15) | copy-start | bytes 6148
  14.5 40.5 %copy-start.5 = (bf16[256]{0:T(256)(128)(2,1)S(1)}, bf16[256]{0:T(256)(128)(2,1)}, u32[]{:S(2)}) copy-start(bf16[256]{0:T(256)(128)(2,1)} %param.11) | copy-start | bytes 1540
  14.5 40.8 %copy-start.4 = (s32[2]{0:T(128)S(1)}, s32[2]{0:T(128)}, u32[]{:S(2)}) copy-start(s32[2]{0:T(128)} %param.12) | copy-start | bytes 28
  46.1 636.9 %all-gather.8.cloned.1.call-start = ((), (), s32[]{:S(2)}) async-start(), calls=%async_computation.6 | async-start | bytes 2129920 | tf_op jit(solution)/shard_map/all_gather | solution.py:64
  49.0 14.5 %all-to-all-start.2 = ((bf16[16,20,128]{2,1,0:T(8,128)(2,1)}), bf16[16,20,128]{2,1,0:T(8,128)(2,1)S(1)}, u32[]{:S(2)}, u32[]{:S(2)}) async-start(bf16[16,20,128]{2,1,0:T(8,128)(2,1)} %broadcast_select_fusion.1), calls=%async_computation.2 | async-start | bytes 196608 | tf_op jit(solution)/shard_map/all_to_all | solution.py:106
  54.9 1029.9 %reduce-scatter.2.cloned.1.call-start = ((), (), s32[]{:S(2)}) async-start(), calls=%async_computation.7 | async-start | bytes 4259840 | tf_op jit(solution)/shard_map/reduce_scatter | solution.py:80
  385.4 315.2 %copy-start.3 = (s32[2]{0:T(128)S(1)}, s32[2]{0:T(128)}, u32[]{:S(2)}) copy-start(s32[2]{0:T(128)} %param.13) | copy-start | bytes 28
Sparse Core Ops, SparseCore 0:
  10.1 305.9 all-gather.5
  318.3 62.2 all-gather.3
  382.7 300.2 all-gather.7
  764.2 320.4 reduce-scatter.1
